TPU v7x, 32 devices: a whole 2x2x4 slice. The times are simulated.
32 devices in a mesh: doc: 8 (over y, x, core), seq: 4 (over z).
Axes of the slice: x: 2, y: 2, z: 4, core: 2. Of those that a mesh axis runs over, the one named last changes fastest.
Arguments:
- images: bfloat16 [8, 4, 128, 8192], P('doc', None, None, 'seq'), may hold values from -6 to 6
- kv_weight: bfloat16 [1024, 8192], P('doc', 'seq'), may hold values from -0.0625 to 0.0625
- q_gain: float32 [128], replicated, may hold values from 0.1 to 1.9
- k_gain: float32 [128], replicated, may hold values from 0.1 to 1.9
- queries: bfloat16 [8, 512, 4096], P('doc', 'seq'), may hold values from -6 to 6
- cotangent: bfloat16 [8, 512, 4096], P('doc', 'seq'), may hold values from -6 to 6
- tile_count: int32 [8], replicated, may hold values from 1 to 4, as said below
- tile_target: int32 [8, 4], replicated, may hold values from 0 to 8, as said below
- tile_source: int32 [8, 4], replicated, may hold values from 0 to 8, as said below
- text_length: int32 [8], replicated, may hold values from 64 to 512, as said below
Outputs:
- attn_out: bfloat16 [8, 512, 4096], P('doc', 'seq')
- kv_weight_grad: float32 [1024, 8192], P('doc', 'seq')
Inputs may be any that keep to these rules, and one draw needn't show every extreme that they name: `tile_count`: some document has 4 tiles and some has 1. `tile_target`: 8 marks an empty slot. The tile in slot k of an encoder device is tile k of its document; no encoder device holds two tiles of one document. Agrees with tile_source and tile_count. `tile_source`: 8 for k at or beyond the document's tile count; otherwise the encoder device that holds tile k in its slot k. `text_length`: live rows come first; some document has all 512 rows live.
All inputs are finite; a program needn't handle non-finite values.
Results may differ from a plain program's by a relative error of at most 0.03.
Values may be sent and summed in bfloat16 or wider, within the bound.
No kernel may reach another device: no remote copies, remote signals or barrier semaphores. Data moves between devices by JAX's collectives and lax.ppermute only.
A program may use at most 64 MiB of HBM per device.

v0:
```python
import math
import jax
import jax.numpy as jnp
from jax import lax
from jax.sharding import PartitionSpec as P

EPS = 1e-05


def cross_core(kv_tiles, query_rows, grad_rows, q_gain, k_gain, key_live, row_live):
    key_width = kv_tiles.shape[-1] // 2
    head_dim = q_gain.shape[0]
    kv_heads = key_width // head_dim
    token_rows = query_rows.shape[0]
    q_heads = query_rows.shape[1] // head_dim
    group_size = q_heads // kv_heads
    inv_root = 1.0 / math.sqrt(head_dim)
    key_raw = kv_tiles[:, :key_width].reshape(-1, kv_heads, head_dim).astype(jnp.float32)
    values = kv_tiles[:, key_width:].reshape(-1, kv_heads, head_dim)
    key_scale = lax.rsqrt(jnp.mean(key_raw * key_raw, axis=-1, keepdims=True) + EPS)
    key_normed = (key_raw * key_scale * k_gain).astype(jnp.bfloat16)
    query_raw = query_rows.reshape(token_rows, kv_heads, group_size, head_dim).astype(jnp.float32)
    query_scale = lax.rsqrt(jnp.mean(query_raw * query_raw, axis=-1, keepdims=True) + EPS)
    query_normed = (query_raw * query_scale * q_gain).astype(jnp.bfloat16)
    row_mask = row_live[:, None, None, None]
    grad_live = grad_rows.reshape(token_rows, kv_heads, group_size, head_dim) * row_mask.astype(
        jnp.bfloat16
    )

    def one_head(items):
        key_head, value_head, query_head, grad_head = items
        scores = (
            jnp.einsum("tgd,ld->tgl", query_head, key_head, preferred_element_type=jnp.float32)
            * inv_root
        )
        expd = jnp.exp(scores) * key_live
        attend = expd / jnp.sum(expd, axis=-1, keepdims=True)
        attend_low = attend.astype(jnp.bfloat16)
        mixed = jnp.einsum(
            "tgl,ld->tgd", attend_low, value_head, preferred_element_type=jnp.float32
        )
        mixed_low = (mixed * row_live[:, None, None]).astype(jnp.bfloat16)
        grad_attend = jnp.einsum(
            "tgd,ld->tgl", grad_head, value_head, preferred_element_type=jnp.float32
        )
        grad_scores = attend * (grad_attend - jnp.sum(attend * grad_attend, axis=-1, keepdims=True))
        grad_low = (grad_scores * inv_root).astype(jnp.bfloat16)
        grad_keyn = jnp.einsum(
            "tgl,tgd->ld", grad_low, query_head, preferred_element_type=jnp.float32
        )
        grad_values = jnp.einsum(
            "tgl,tgd->ld", attend_low, grad_head, preferred_element_type=jnp.float32
        )
        return (mixed_low, grad_keyn, grad_values)

    head_items = (
        jnp.moveaxis(key_normed, 1, 0),
        jnp.moveaxis(values, 1, 0),
        jnp.moveaxis(query_normed, 1, 0),
        jnp.moveaxis(grad_live, 1, 0),
    )
    mixed_heads, keyn_heads, value_heads = lax.map(one_head, head_items)
    attn_rows = jnp.moveaxis(mixed_heads, 0, 1).reshape(token_rows, -1)
    grad_keyn = jnp.moveaxis(keyn_heads, 0, 1)
    grad_values = jnp.moveaxis(value_heads, 0, 1)
    weighted = grad_keyn * k_gain
    cubed = key_scale * key_scale * key_scale
    grad_keys = key_scale * weighted - key_raw * cubed * jnp.mean(
        weighted * key_raw, axis=-1, keepdims=True
    )
    grad_kv = jnp.concatenate(
        [grad_keys.reshape(-1, key_width), grad_values.reshape(-1, key_width)], axis=-1
    )
    return (attn_rows, grad_kv)


def per_device(
    images,
    kv_weight,
    q_gain,
    k_gain,
    queries,
    cotangent,
    tile_count,
    tile_target,
    tile_source,
    text_length,
):
    n_doc = lax.axis_size("doc")
    n_seq = lax.axis_size("seq")
    doc_at = lax.axis_index("doc")
    seq_at = lax.axis_index("seq")
    slots = images.shape[1]
    tile_rows = images.shape[2]
    part_rows = tile_rows // n_seq
    own_cols = images[0].reshape(slots * tile_rows, images.shape[3])
    partial_value = lax.dot_general(
        own_cols,
        lax.all_gather(kv_weight, "doc", axis=0, tiled=True),
        (((1,), (1,)), ((), ())),
        preferred_element_type=jnp.float32,
    )
    width = partial_value.shape[1]
    partial_value = partial_value.reshape(slots, tile_rows, width)
    summed = lax.psum(partial_value.astype(jnp.bfloat16), "seq").astype(jnp.float32)
    own_share = lax.dynamic_slice_in_dim(summed, seq_at * part_rows, part_rows, 1)
    kv_own = own_share.astype(jnp.bfloat16)
    doc_ids = jnp.arange(n_doc, dtype=jnp.int32)
    slot_ids = jnp.arange(slots, dtype=jnp.int32)
    targets = tile_target[doc_at]
    send_map = (targets[None, :] == doc_ids[:, None]).astype(jnp.bfloat16)
    outgoing = jnp.einsum(
        "ds,src->drc", send_map, kv_own, preferred_element_type=jnp.float32
    ).astype(jnp.bfloat16)
    incoming = lax.all_to_all(outgoing, "doc", split_axis=0, concat_axis=0, tiled=True)
    tiles_here = tile_count[doc_at]
    sources = tile_source[doc_at]
    live_slot = slot_ids < tiles_here
    pick_map = ((sources[:, None] == doc_ids[None, :]) & live_slot[:, None]).astype(jnp.bfloat16)
    kv_part = jnp.einsum(
        "se,erc->src", pick_map, incoming, preferred_element_type=jnp.float32
    ).astype(jnp.bfloat16)
    kv_full = lax.all_gather(kv_part, "seq", axis=1, tiled=True)
    token_rows = queries.shape[1]
    key_live = (jnp.arange(slots * tile_rows, dtype=jnp.int32) // tile_rows < tiles_here).astype(
        jnp.float32
    )
    row_index = seq_at * token_rows + jnp.arange(token_rows, dtype=jnp.int32)
    row_live = (row_index < text_length[doc_at]).astype(jnp.float32)
    attn_rows, grad_kv = cross_core(
        kv_full.reshape(slots * tile_rows, width),
        queries[0],
        cotangent[0],
        q_gain,
        k_gain,
        key_live,
        row_live,
    )
    attn_out = attn_rows[None]
    grad_kv = grad_kv.reshape(slots, tile_rows, width)
    grad_sum = lax.psum(grad_kv.astype(jnp.bfloat16), "seq").astype(jnp.float32)
    grad_share = lax.dynamic_slice_in_dim(grad_sum, seq_at * part_rows, part_rows, 1)
    grad_own = grad_share.astype(jnp.bfloat16)
    back_out = jnp.einsum(
        "se,src->erc", pick_map, grad_own, preferred_element_type=jnp.float32
    ).astype(jnp.bfloat16)
    back_in = lax.all_to_all(back_out, "doc", split_axis=0, concat_axis=0, tiled=True)
    returned = jnp.einsum(
        "ds,drc->src", send_map, back_in, preferred_element_type=jnp.float32
    ).astype(jnp.bfloat16)
    grad_full = lax.all_gather(returned, "seq", axis=1, tiled=True)
    grad_flat = grad_full.reshape(slots * tile_rows, width)
    rows_each = width // n_doc
    weight_part = lax.dot_general(
        grad_flat, own_cols, (((0,), (0,)), ((), ())), preferred_element_type=jnp.float32
    )
    weight_sum = lax.psum(weight_part.astype(jnp.bfloat16), "doc").astype(jnp.float32)
    weight_grad = lax.dynamic_slice_in_dim(weight_sum, doc_at * rows_each, rows_each, 0)
    return (attn_out, weight_grad)


def solution(mesh):
    return jax.shard_map(
        per_device,
        mesh=mesh,
        in_specs=(
            P("doc", None, None, "seq"),
            P("doc", "seq"),
            P(),
            P(),
            P("doc", "seq", None),
            P("doc", "seq", None),
            P(),
            P(),
            P(),
            P(),
        ),
        out_specs=(P("doc", "seq", None), P("doc", "seq")),
        check_vma=False,
    )
```

profile of v0, /device:TPU:0, one launch (start us, length us, event | category | flops | bytes accessed | tf_op | source)
XLA Modules:
  0.0 441.7 jit_solution(6251067855293527332)
XLA Ops:
  8.0 41.2 %all-gather.4.cloned.1.call-done = bf16[1024,2048]{1,0:T(8,128)(2,1)} async-done(((bf16[128,2048]{1,0:T(8,128)(2,1)}), bf16[1024,2048]{1,0:T(8,128)(2,1)}) %all-gather.4.cloned.1.call-update) | async-done | bytes 4194320 | tf_op jit(solution)/shard_map/all_gather | solution.py:99
  49.2 5.5 %fusion.64 = bf16[4,128,1024]{2,1,0:T(8,128)(2,1)} fusion(bf16[1024,2048]{1,0:T(8,128)(2,1)} %all-gather.4.cloned.1.call-done, bf16[1,4,128,2048]{3,2,1,0:T(8,128)(2,1)S(1)} %copy-done), kind=kOutput, calls=%fused_computation.63 | convolution fusion | flops 2148007936 | bytes 7340032 | tf_op jit(solution)/shard_map/dot_general | solution.py:97
  55.0 51.8 %all-reduce.4.cloned.1.call-done = bf16[4,128,1024]{2,1,0:T(8,128)(2,1)} async-done(((bf16[4,128,1024]{2,1,0:T(8,128)(2,1)}), bf16[4,128,1024]{2,1,0:T(8,128)(2,1)}) %all-reduce.4.cloned.1.call-update) | async-done | bytes 1048592 | tf_op jit(solution)/shard_map/psum | solution.py:105
  109.3 3.7 all-to-all-start
  114.5 8.2 %all-to-all-done = bf16[8,32,1024]{2,1,0:T(8,128)(2,1)S(1)} async-done(((bf16[8,32,1024]{2,1,0:T(8,128)(2,1)}), bf16[8,32,1024]{2,1,0:T(8,128)(2,1)S(1)}, u32[]{:S(2)}, u32[]{:S(2)}) %all-to-all-start) | async-done | bytes 524320 | tf_op jit(solution)/shard_map/all_to_all | solution.py:115
  133.3 16.2 %all-gather.6.cloned.1.call-done = bf16[4,128,1024]{2,0,1:T(4,128)(2,1)} async-done(((bf16[4,32,1024]{2,0,1:T(4,128)(2,1)}), bf16[4,128,1024]{2,0,1:T(4,128)(2,1)}) %all-gather.6.cloned.1.call-update) | async-done | bytes 1048592 | tf_op jit(solution)/shard_map/all_gather | solution.py:123
  157.1 87.8 %while.15 = (s32[]{:T(128)}, bf16[4,128,8,128]{3,1,2,0:T(8,128)(2,1)}, f32[4,512,128]{1,2,0:T(8,128)}, bf16[4,512,128]{2,1,0:T(8,128)(2,1)}, bf16[4,128,8,128]{1...) while((s32[]{:T(128)}, ...), condition=%wide.region_6.7_spmd.clone, body=%wide.region_3.6_spmd.clone.sunk | while | flops 682891136 | bytes 27433116 | solution.py:62
  157.7 2.8 fusion.115
  163.2 9.8 %fusion.118 = f32[4,512,128]{1,2,0:T(8,128)} fusion(f32[4,512,128]{1,2,0:T(8,128)} %get-tuple-element.222, s32[]{:T(128)} %get-tuple-element.220, f32[128,8,512]{2,0,1:T(8,128)} %fusion.117, bf16[4,128,8,128]{1,3,2,0:T(8,128)(2,1)} %get-tuple-element.236, f32[128,8,512]{2,0,1:T(8,128)} %get-tuple-element.206, f32[128,8]{0,1:T(8,128)S(1)} %get-tuple-element.207, ...), kind=kOutput, calls=%fused_computation.13.clone.1 | convolution fusion | flops 139986432 | bytes 8926208 | tf_op jit(solution)/shard_map/while/body/eval_jaxpr/tgl,tgd->ld/dot_general | solution.py:48
  173.0 3.1 fusion.119
  179.6 2.8 fusion.115
  185.2 9.8 %fusion.118 = f32[4,512,128]{1,2,0:T(8,128)} fusion(f32[4,512,128]{1,2,0:T(8,128)} %get-tuple-element.222, s32[]{:T(128)} %get-tuple-element.220, f32[128,8,512]{2,0,1:T(8,128)} %fusion.117, bf16[4,128,8,128]{1,3,2,0:T(8,128)(2,1)} %get-tuple-element.236, f32[128,8,512]{2,0,1:T(8,128)} %get-tuple-element.206, f32[128,8]{0,1:T(8,128)S(1)} %get-tuple-element.207, ...), kind=kOutput, calls=%fused_computation.13.clone.1 | convolution fusion | flops 139986432 | bytes 8926208 | tf_op jit(solution)/shard_map/while/body/eval_jaxpr/tgl,tgd->ld/dot_general | solution.py:48
  195.0 3.1 fusion.119
  201.6 2.8 fusion.115
  207.1 9.8 %fusion.118 = f32[4,512,128]{1,2,0:T(8,128)} fusion(f32[4,512,128]{1,2,0:T(8,128)} %get-tuple-element.222, s32[]{:T(128)} %get-tuple-element.220, f32[128,8,512]{2,0,1:T(8,128)} %fusion.117, bf16[4,128,8,128]{1,3,2,0:T(8,128)(2,1)} %get-tuple-element.236, f32[128,8,512]{2,0,1:T(8,128)} %get-tuple-element.206, f32[128,8]{0,1:T(8,128)S(1)} %get-tuple-element.207, ...), kind=kOutput, calls=%fused_computation.13.clone.1 | convolution fusion | flops 139986432 | bytes 8926208 | tf_op jit(solution)/shard_map/while/body/eval_jaxpr/tgl,tgd->ld/dot_general | solution.py:48
  216.9 3.1 fusion.119
  223.5 2.8 fusion.115
  229.0 9.8 %fusion.118 = f32[4,512,128]{1,2,0:T(8,128)} fusion(f32[4,512,128]{1,2,0:T(8,128)} %get-tuple-element.222, s32[]{:T(128)} %get-tuple-element.220, f32[128,8,512]{2,0,1:T(8,128)} %fusion.117, bf16[4,128,8,128]{1,3,2,0:T(8,128)(2,1)} %get-tuple-element.236, f32[128,8,512]{2,0,1:T(8,128)} %get-tuple-element.206, f32[128,8]{0,1:T(8,128)S(1)} %get-tuple-element.207, ...), kind=kOutput, calls=%fused_computation.13.clone.1 | convolution fusion | flops 139986432 | bytes 8926208 | tf_op jit(solution)/shard_map/while/body/eval_jaxpr/tgl,tgd->ld/dot_general | solution.py:48
  238.9 3.1 fusion.119
  253.5 51.4 %all-reduce.6.cloned.1.call-done = bf16[4,128,1024]{2,0,1:T(4,128)(2,1)} async-done(((bf16[4,128,1024]{2,0,1:T(4,128)(2,1)}), bf16[4,128,1024]{2,0,1:T(4,128)(2,1)}) %all-reduce.6.cloned.1.call-update) | async-done | bytes 1048592 | tf_op jit(solution)/shard_map/psum | solution.py:141
  306.5 13.2 %all_to_all.10 = bf16[8,32,1024]{2,1,0:T(8,128)(2,1)S(1)} all-to-all(bf16[8,32,1024]{2,1,0:T(8,128)(2,1)S(1)} %copy.51), channel_id=1, replica_groups=mesh['doc'=8,'seq'=4] {'doc'}, dimensions={0} | all-to-all | bytes 1048576 | tf_op jit(solution)/shard_map/all_to_all | solution.py:147
  321.1 25.3 %all-gather.8.cloned.1.call-done = bf16[4,128,1024]{2,0,1:T(4,128)(2,1)} async-done(((bf16[4,32,1024]{2,0,1:T(4,128)(2,1)}), bf16[4,128,1024]{2,0,1:T(4,128)(2,1)}) %all-gather.8.cloned.1.call-update) | async-done | bytes 1048592 | tf_op jit(solution)/shard_map/all_gather | solution.py:151
  348.0 4.4 convolution_convert_fusion
  355.6 77.2 %all-reduce.8.cloned.1.call-done = bf16[1024,2048]{1,0:T(8,128)(2,1)} async-done(((bf16[1024,2048]{1,0:T(8,128)(2,1)}), bf16[1024,2048]{1,0:T(8,128)(2,1)}) %all-reduce.8.cloned.1.call-update) | async-done | bytes 4194320 | tf_op jit(solution)/shard_map/psum | solution.py:157
  (96 shorter events, 66.4 us)
Async XLA Ops:
  7.2 42.1 %copy-start = (bf16[1,4,128,2048]{3,2,1,0:T(8,128)(2,1)S(1)}, bf16[1,4,128,2048]{3,2,1,0:T(8,128)(2,1)}, u32[]{:S(2)}) copy-start(bf16[1,4,128,2048]{3,2,1,0:T(8,128)(2,1)} %param.12) | copy-start | bytes 6291460
  7.2 42.0 %all-gather.4.cloned.1.call-start = ((), (), s32[]{:S(2)}) async-start(), calls=%async_computation.2 | async-start | bytes 4718592 | tf_op jit(solution)/shard_map/all_gather | solution.py:99
  7.9 46.9 %copy-start.5 = (s32[8,4]{0,1:T(4,128)S(1)}, s32[8,4]{0,1:T(4,128)}, u32[]{:S(2)}) copy-start(s32[8,4]{0,1:T(4,128)} %param.19) | copy-start | bytes 388
  7.9 98.9 %all-reduce.4.cloned.1.call-start = ((), (), s32[]{:S(2)}) async-start(), calls=%async_computation.3 | async-start | bytes 2097152 | tf_op jit(solution)/shard_map/psum | solution.py:105
  54.7 58.3 %copy-start.8 = (s32[8]{0:T(128)S(1)}, s32[8]{0:T(128)}, u32[]{:S(2)}) copy-start(s32[8]{0:T(128)} %param.18) | copy-start | bytes 100
  54.7 58.9 %copy-start.6 = (s32[8,4]{0,1:T(4,128)S(1)}, s32[8,4]{0,1:T(4,128)}, u32[]{:S(2)}) copy-start(s32[8,4]{0,1:T(4,128)} %param.20) | copy-start | bytes 388
  107.8 16.3 %copy-start.9 = (s32[8]{0:T(128)S(1)}, s32[8]{0:T(128)}, u32[]{:S(2)}) copy-start(s32[8]{0:T(128)} %param.21) | copy-start | bytes 100
  109.3 13.4 %all-to-all-start = ((bf16[8,32,1024]{2,1,0:T(8,128)(2,1)}), bf16[8,32,1024]{2,1,0:T(8,128)(2,1)S(1)}, u32[]{:S(2)}, u32[]{:S(2)}) async-start(bf16[8,32,1024]{2,1,0:T(8,128)(2,1)} %copy.35), calls=%async_computation | async-start | bytes 1048576 | tf_op jit(solution)/shard_map/all_to_all | solution.py:115
  113.0 36.5 %all-gather.6.cloned.1.call-start = ((), (), s32[]{:S(2)}) async-start(), calls=%async_computation.4 | async-start | bytes 1310720 | tf_op jit(solution)/shard_map/all_gather | solution.py:123
  123.9 181.0 %all-reduce.6.cloned.1.call-start = ((), (), s32[]{:S(2)}) async-start(), calls=%async_computation.5 | async-start | bytes 2097152 | tf_op jit(solution)/shard_map/psum | solution.py:141
  128.7 3.2 copy-start.7
  152.3 3.8 copy-start.4
  173.0 3.7 copy-start.1
  195.0 3.7 copy-start.1
  216.9 3.7 copy-start.1
  238.9 3.7 copy-start.1
  244.8 1.5 copy-start.2
  247.5 2.4 copy-start.3
  253.4 93.0 %all-gather.8.cloned.1.call-start = ((), (), s32[]{:S(2)}) async-start(), calls=%async_computation.6 | async-start | bytes 1310720 | tf_op jit(solution)/shard_map/all_gather | solution.py:151
  320.9 111.9 %all-reduce.8.cloned.1.call-start = ((), (), s32[]{:S(2)}) async-start(), calls=%async_computation.7 | async-start | bytes 8388608 | tf_op jit(solution)/shard_map/psum | solution.py:157
Sparse Core Ops, SparseCore 0:
  9.9 39.2 all-gather.3
  54.9 51.8 all-reduce.3
  124.0 25.4 all-gather.5
  253.6 51.2 all-reduce.5
  321.0 25.4 all-gather.7
  352.5 80.1 all-reduce.7
where the time goes:
time: 443 us; the launch traced here: 442 us
  waiting for transfers between devices  272 us (61%)
  matrix products  96.6 us (22%)
  other arithmetic  20.8 us (5%)
  local copies, waits for them, and re-layouts  20.3 us (5%)
  between operations  14.3 us (3%)
  blocking collectives  13.2 us (3%)
    psum x1, waiting for transfers between devices, per_device(): lax.psum(weight_part.astype(jnp.bfloat16), 'doc').astype(jnp.float32)  77.2 us
    psum x1, waiting for transfers between devices, per_device(): lax.psum(partial_value.astype(jnp.bfloat16), 'seq').astype(jnp.float32)  51.8 us
    psum x1, waiting for transfers between devices, per_device(): grad_sum = lax.psum(grad_kv.astype(jnp.bfloat16), 'seq').astype(jnp.float32)  51.4 us
    all_gather x1, waiting for transfers between devices, per_device(): lax.all_gather(kv_weight, 'doc', axis=0, tiled=True)  41.2 us
    dot_general x4, matrix products, one_head(): jnp.einsum('tgl,tgd->ld', grad_low, query_head, preferred_element_type=jn...  39.3 us
    all_gather x1, waiting for transfers between devices, per_device(): grad_full = lax.all_gather(returned, 'seq', axis=1, tiled=True)  25.3 us
    all_gather x1, waiting for transfers between devices, per_device(): kv_full = lax.all_gather(kv_part, 'seq', axis=1, tiled=True)  16.2 us
    all_to_all x1, blocking collectives, per_device(): lax.all_to_all(back_out, 'doc', split_axis=0, concat_axis=0, tiled=True)  13.2 us
  transfers between devices with their start and end apart: 7, of which 7 were waited for; matrix products, arithmetic and copies ran while one was open for 3% of the time, Pallas kernels for 0%

commit v1 on v0

--- a/solution.py
+++ b/solution.py
@@ -138,7 +138,9 @@
     )
     attn_out = attn_rows[None]
     grad_kv = grad_kv.reshape(slots, tile_rows, width)
-    grad_sum = lax.psum(grad_kv.astype(jnp.bfloat16), "seq").astype(jnp.float32)
+    grad_sum = jnp.sum(lax.all_gather(grad_kv.astype(jnp.bfloat16), "seq"), axis=0).astype(
+        jnp.float32
+    )
     grad_share = lax.dynamic_slice_in_dim(grad_sum, seq_at * part_rows, part_rows, 1)
     grad_own = grad_share.astype(jnp.bfloat16)
     back_out = jnp.einsum(

time: 443 us -> 474 us (1.070)
  waiting for transfers between devices: 272 us -> 300 us
    all_gather x0 -> x1, waiting for transfers between devices: none -> 80.2 us  [per_device(): lax.all_gather(grad_kv.astype(jnp.bfloat16), 'seq')]
    psum x1 -> x0, waiting for transfers between devices: 51.4 us -> none  [per_device(): grad_sum = lax.psum(grad_kv.astype(jnp.bfloat16), 'seq').astype(jnp.float32)]
where the time goes in v1:
time: 474 us; the launch traced here: 473 us
  waiting for transfers between devices  300 us (63%)
  matrix products  95.8 us (20%)
  other arithmetic  24.4 us (5%)
  local copies, waits for them, and re-layouts  20.8 us (4%)
  between operations  14.3 us (3%)
  blocking collectives  13.2 us (3%)
    all_gather x1, waiting for transfers between devices, per_device(): lax.all_gather(grad_kv.astype(jnp.bfloat16), 'seq')  80.2 us
    psum x1, waiting for transfers between devices, per_device(): lax.psum(weight_part.astype(jnp.bfloat16), 'doc').astype(jnp.float32)  77.2 us
    psum x1, waiting for transfers between devices, per_device(): lax.psum(partial_value.astype(jnp.bfloat16), 'seq').astype(jnp.float32)  51.8 us
    all_gather x1, waiting for transfers between devices, per_device(): lax.all_gather(kv_weight, 'doc', axis=0, tiled=True)  41.2 us
    dot_general x4, matrix products, one_head(): jnp.einsum('tgl,tgd->ld', grad_low, query_head, preferred_element_type=jn...  39.3 us
    all_gather x1, waiting for transfers between devices, per_device(): grad_full = lax.all_gather(returned, 'seq', axis=1, tiled=True)  24.5 us
    all_gather x1, waiting for transfers between devices, per_device(): kv_full = lax.all_gather(kv_part, 'seq', axis=1, tiled=True)  16.1 us
    all_to_all x1, blocking collectives, per_device(): lax.all_to_all(back_out, 'doc', split_axis=0, concat_axis=0, tiled=True)  13.2 us
  transfers between devices with their start and end apart: 7, of which 7 were waited for; matrix products, arithmetic and copies ran while one was open for 3% of the time, Pallas kernels for 0%

profile of v1, /device:TPU:0, one launch (start us, length us, event | category | flops | bytes accessed | tf_op | source)
XLA Modules:
  0.0 472.9 jit_solution(7830801002838572219)
XLA Ops:
  8.0 41.2 %all-gather.5.cloned.1.call-done = bf16[1024,2048]{1,0:T(8,128)(2,1)} async-done(((bf16[128,2048]{1,0:T(8,128)(2,1)}), bf16[1024,2048]{1,0:T(8,128)(2,1)}) %all-gather.5.cloned.1.call-update) | async-done | bytes 4194320 | tf_op jit(solution)/shard_map/all_gather | solution.py:99
  49.2 5.5 %fusion.64 = bf16[4,128,1024]{2,1,0:T(8,128)(2,1)} fusion(bf16[1024,2048]{1,0:T(8,128)(2,1)} %all-gather.5.cloned.1.call-done, bf16[1,4,128,2048]{3,2,1,0:T(8,128)(2,1)S(1)} %copy-done), kind=kOutput, calls=%fused_computation.63 | convolution fusion | flops 2148007936 | bytes 7340032 | tf_op jit(solution)/shard_map/dot_general | solution.py:97
  55.0 51.8 %all-reduce.3.cloned.1.call-done = bf16[4,128,1024]{2,1,0:T(8,128)(2,1)} async-done(((bf16[4,128,1024]{2,1,0:T(8,128)(2,1)}), bf16[4,128,1024]{2,1,0:T(8,128)(2,1)}) %all-reduce.3.cloned.1.call-update) | async-done | bytes 1048592 | tf_op jit(solution)/shard_map/psum | solution.py:105
  109.3 3.7 all-to-all-start
  114.6 8.1 %all-to-all-done = bf16[8,32,1024]{2,1,0:T(8,128)(2,1)S(1)} async-done(((bf16[8,32,1024]{2,1,0:T(8,128)(2,1)}), bf16[8,32,1024]{2,1,0:T(8,128)(2,1)S(1)}, u32[]{:S(2)}, u32[]{:S(2)}) %all-to-all-start) | async-done | bytes 524320 | tf_op jit(solution)/shard_map/all_to_all | solution.py:115
  133.3 16.1 %all-gather.7.cloned.1.call-done = bf16[4,128,1024]{2,0,1:T(4,128)(2,1)} async-done(((bf16[4,32,1024]{2,0,1:T(4,128)(2,1)}), bf16[4,128,1024]{2,0,1:T(4,128)(2,1)}) %all-gather.7.cloned.1.call-update) | async-done | bytes 1048592 | tf_op jit(solution)/shard_map/all_gather | solution.py:123
  157.0 88.4 %while.15 = (s32[]{:T(128)}, bf16[4,128,8,128]{3,1,2,0:T(8,128)(2,1)}, f32[4,512,128]{1,2,0:T(8,128)}, bf16[4,512,128]{2,1,0:T(8,128)(2,1)}, bf16[4,128,8,128]{1...) while((s32[]{:T(128)}, ...), condition=%wide.region_6.7_spmd.clone, body=%wide.region_3.6_spmd.clone.sunk | while | flops 682891136 | bytes 27433116 | solution.py:62
  157.7 2.8 fusion.114
  163.3 9.8 %fusion.117 = f32[4,512,128]{1,2,0:T(8,128)} fusion(f32[4,512,128]{1,2,0:T(8,128)} %get-tuple-element.244, s32[]{:T(128)} %get-tuple-element.242, f32[128,8,512]{2,0,1:T(8,128)} %fusion.116, bf16[4,128,8,128]{1,3,2,0:T(8,128)(2,1)} %get-tuple-element.258, f32[128,8,512]{2,0,1:T(8,128)} %get-tuple-element.228, f32[128,8]{0,1:T(8,128)S(1)} %get-tuple-element.229, ...), kind=kOutput, calls=%fused_computation.13.clone.1 | convolution fusion | flops 139986432 | bytes 8926208 | tf_op jit(solution)/shard_map/while/body/eval_jaxpr/tgl,tgd->ld/dot_general | solution.py:48
  173.1 3.1 fusion.118
  179.8 2.8 fusion.114
  185.4 9.8 %fusion.117 = f32[4,512,128]{1,2,0:T(8,128)} fusion(f32[4,512,128]{1,2,0:T(8,128)} %get-tuple-element.244, s32[]{:T(128)} %get-tuple-element.242, f32[128,8,512]{2,0,1:T(8,128)} %fusion.116, bf16[4,128,8,128]{1,3,2,0:T(8,128)(2,1)} %get-tuple-element.258, f32[128,8,512]{2,0,1:T(8,128)} %get-tuple-element.228, f32[128,8]{0,1:T(8,128)S(1)} %get-tuple-element.229, ...), kind=kOutput, calls=%fused_computation.13.clone.1 | convolution fusion | flops 139986432 | bytes 8926208 | tf_op jit(solution)/shard_map/while/body/eval_jaxpr/tgl,tgd->ld/dot_general | solution.py:48
  195.2 3.1 fusion.118
  207.4 9.8 %fusion.117 = f32[4,512,128]{1,2,0:T(8,128)} fusion(f32[4,512,128]{1,2,0:T(8,128)} %get-tuple-element.244, s32[]{:T(128)} %get-tuple-element.242, f32[128,8,512]{2,0,1:T(8,128)} %fusion.116, bf16[4,128,8,128]{1,3,2,0:T(8,128)(2,1)} %get-tuple-element.258, f32[128,8,512]{2,0,1:T(8,128)} %get-tuple-element.228, f32[128,8]{0,1:T(8,128)S(1)} %get-tuple-element.229, ...), kind=kOutput, calls=%fused_computation.13.clone.1 | convolution fusion | flops 139986432 | bytes 8926208 | tf_op jit(solution)/shard_map/while/body/eval_jaxpr/tgl,tgd->ld/dot_general | solution.py:48
  217.3 3.1 fusion.118
  224.0 2.8 fusion.114
  229.5 9.8 %fusion.117 = f32[4,512,128]{1,2,0:T(8,128)} fusion(f32[4,512,128]{1,2,0:T(8,128)} %get-tuple-element.244, s32[]{:T(128)} %get-tuple-element.242, f32[128,8,512]{2,0,1:T(8,128)} %fusion.116, bf16[4,128,8,128]{1,3,2,0:T(8,128)(2,1)} %get-tuple-element.258, f32[128,8,512]{2,0,1:T(8,128)} %get-tuple-element.228, f32[128,8]{0,1:T(8,128)S(1)} %get-tuple-element.229, ...), kind=kOutput, calls=%fused_computation.13.clone.1 | convolution fusion | flops 139986432 | bytes 8926208 | tf_op jit(solution)/shard_map/while/body/eval_jaxpr/tgl,tgd->ld/dot_general | solution.py:48
  239.4 3.1 fusion.118
  254.2 80.2 %all-gather.9.cloned.1.call-done = bf16[4,4,128,1024]{3,2,1,0:T(8,128)(2,1)} async-done(((bf16[1,4,128,1024]{3,2,1,0:T(8,128)(2,1)}), bf16[4,4,128,1024]{3,2,1,0:T(8,128)(2,1)}) %all-gather.9.cloned.1.call-update) | async-done | bytes 4194320 | tf_op jit(solution)/shard_map/all_gather | solution.py:141
  334.4 3.3 reduce_sum.60
  338.5 13.2 %all_to_all.10 = bf16[8,32,1024]{2,1,0:T(8,128)(2,1)S(1)} all-to-all(bf16[8,32,1024]{2,1,0:T(8,128)(2,1)S(1)} %copy.93), channel_id=1, replica_groups=mesh['doc'=8,'seq'=4] {'doc'}, dimensions={0} | all-to-all | bytes 1048576 | tf_op jit(solution)/shard_map/all_to_all | solution.py:149
  353.1 24.5 %all-gather.11.cloned.1.call-done = bf16[4,128,1024]{2,0,1:T(4,128)(2,1)} async-done(((bf16[4,32,1024]{2,0,1:T(4,128)(2,1)}), bf16[4,128,1024]{2,0,1:T(4,128)(2,1)}) %all-gather.11.cloned.1.call-update) | async-done | bytes 1048592 | tf_op jit(solution)/shard_map/all_gather | solution.py:153
  379.2 4.4 convolution_convert_fusion
  386.8 77.2 %all-reduce.5.cloned.1.call-done = bf16[1024,2048]{1,0:T(8,128)(2,1)} async-done(((bf16[1024,2048]{1,0:T(8,128)(2,1)}), bf16[1024,2048]{1,0:T(8,128)(2,1)}) %all-reduce.5.cloned.1.call-update) | async-done | bytes 4194320 | tf_op jit(solution)/shard_map/psum | solution.py:159
  (95 shorter events, 69.1 us)
Async XLA Ops:
  7.2 42.1 %copy-start = (bf16[1,4,128,2048]{3,2,1,0:T(8,128)(2,1)S(1)}, bf16[1,4,128,2048]{3,2,1,0:T(8,128)(2,1)}, u32[]{:S(2)}) copy-start(bf16[1,4,128,2048]{3,2,1,0:T(8,128)(2,1)} %param.12) | copy-start | bytes 6291460
  7.2 42.0 %all-gather.5.cloned.1.call-start = ((), (), s32[]{:S(2)}) async-start(), calls=%async_computation.2 | async-start | bytes 4718592 | tf_op jit(solution)/shard_map/all_gather | solution.py:99
  7.9 46.9 %copy-start.4 = (s32[8,4]{0,1:T(4,128)S(1)}, s32[8,4]{0,1:T(4,128)}, u32[]{:S(2)}) copy-start(s32[8,4]{0,1:T(4,128)} %param.19) | copy-start | bytes 388
  7.9 98.9 %all-reduce.3.cloned.1.call-start = ((), (), s32[]{:S(2)}) async-start(), calls=%async_computation.3 | async-start | bytes 2097152 | tf_op jit(solution)/shard_map/psum | solution.py:105
  54.7 58.3 %copy-start.7 = (s32[8]{0:T(128)S(1)}, s32[8]{0:T(128)}, u32[]{:S(2)}) copy-start(s32[8]{0:T(128)} %param.18) | copy-start | bytes 100
  54.7 59.0 %copy-start.5 = (s32[8,4]{0,1:T(4,128)S(1)}, s32[8,4]{0,1:T(4,128)}, u32[]{:S(2)}) copy-start(s32[8,4]{0,1:T(4,128)} %param.20) | copy-start | bytes 388
  107.8 16.3 %copy-start.8 = (s32[8]{0:T(128)S(1)}, s32[8]{0:T(128)}, u32[]{:S(2)}) copy-start(s32[8]{0:T(128)} %param.21) | copy-start | bytes 100
  109.3 13.4 %all-to-all-start = ((bf16[8,32,1024]{2,1,0:T(8,128)(2,1)}), bf16[8,32,1024]{2,1,0:T(8,128)(2,1)S(1)}, u32[]{:S(2)}, u32[]{:S(2)}) async-start(bf16[8,32,1024]{2,1,0:T(8,128)(2,1)} %copy.78), calls=%async_computation | async-start | bytes 1048576 | tf_op jit(solution)/shard_map/all_to_all | solution.py:115
  113.0 36.5 %all-gather.7.cloned.1.call-start = ((), (), s32[]{:S(2)}) async-start(), calls=%async_computation.4 | async-start | bytes 1310720 | tf_op jit(solution)/shard_map/all_gather | solution.py:123
  123.9 210.5 %all-gather.9.cloned.1.call-start = ((), (), s32[]{:S(2)}) async-start(), calls=%async_computation.5 | async-start | bytes 5242880 | tf_op jit(solution)/shard_map/all_gather | solution.py:141
  128.7 3.2 copy-start.6
  152.3 3.8 copy-start.3
  173.1 3.8 copy-start.1
  195.2 3.8 copy-start.1
  217.3 3.8 copy-start.1
  239.3 3.8 copy-start.1
  245.4 1.5 copy-start.2
  254.1 123.5 %all-gather.11.cloned.1.call-start = ((), (), s32[]{:S(2)}) async-start(), calls=%async_computation.6 | async-start | bytes 1310720 | tf_op jit(solution)/shard_map/all_gather | solution.py:153
  352.8 111.1 %all-reduce.5.cloned.1.call-start = ((), (), s32[]{:S(2)}) async-start(), calls=%async_computation.7 | async-start | bytes 8388608 | tf_op jit(solution)/shard_map/psum | solution.py:159
Sparse Core Ops, SparseCore 0:
  9.9 39.2 all-gather.4
  54.9 51.8 all-reduce.2
  124.0 25.4 all-gather.6
  254.2 80.1 all-gather.8
  353.0 24.6 all-gather.10
  383.7 80.1 all-reduce.4
